TPU v7x, 32 devices: a whole 2x2x4 slice. The times are simulated.
32 devices in a mesh: row: 2 (over x), col: 4 (over z), fit: 4 (over y, core).
Axes of the slice: x: 2, y: 2, z: 4, core: 2. Of those that a mesh axis runs over, the one named last changes fastest.
Arguments:
- orbital_ints: bfloat16 [16, 40, 2560], P(('row', 'col'), None, 'fit'), may hold values from -0.83984375 to 0.83984375
- occ_energy: float32 [16], P(('row', 'col')), may hold values from -1.2 to -0.3
- pair_row: int32 [1024], P(('row', 'col')), may hold values from 0 to 7
- pair_col: int32 [1024], P(('row', 'col')), may hold values from 0 to 3
- virt_energy: float32 [40, 1024], P(None, ('row', 'col')), may hold values from 0.5 to 3
- amplitudes: float32 [40, 40, 1024], P(None, None, ('row', 'col')), may hold values from -1.8 to 1.8
- intersections: bfloat16 [40, 40, 16, 1024], P(None, None, 'fit', ('row', 'col')), may hold values from -1 to 1
- coupling_fock: float32 [16, 1024], P('fit', ('row', 'col')), may hold values from -0.25 to 0.25
- partner_owner: int32 [4, 1024, 4], P('fit', ('row', 'col')), may hold values from 0 to 7, all different within a row; in each aligned block of 128 rows (0 to 127, 128 to 255, ..., all dimensions but the last counted through in order) at most 128 rows name the same one
- partner_slot: int32 [4, 1024, 4], P('fit', ('row', 'col')), may hold values from 0 to 127
Outputs:
- new_amplitudes: float32 [40, 40, 1024], P(None, None, ('row', 'col'))
- residual: float32 [40, 40, 1024], P(None, None, ('row', 'col'))
Inputs may be any that keep to these rules, and one draw needn't show every extreme that they name: `partner_owner`: the 4 owners of one pair in one fit index differ; among the pairs of one group in one fit index (aligned blocks of 128 rows) no owner is named more than 128 times, a bound that some block reaches.
All inputs are finite; a program needn't handle non-finite values.
Results may differ from a plain program's by a relative error of at most 0.014.
Values may be sent and summed in bfloat16 or wider, within the bound.
A program may use at most 128 MiB of HBM per device.

v0:
```python
import math
import jax
import jax.numpy as jnp
from jax import lax
from jax.sharding import PartitionSpec as P

ITERS = 2


def on_device(
    orbital_ints,
    occ_energy,
    pair_row,
    pair_col,
    virt_energy,
    amplitudes,
    intersections,
    coupling_fock,
    partner_owner,
    partner_slot,
):
    row_count = lax.axis_size("row")
    col_count = lax.axis_size("col")
    group_count = row_count * col_count
    tile_size = amplitudes.shape[0]
    pair_count = amplitudes.shape[2]
    link_count = partner_owner.shape[2]
    capacity = 2 * pair_count * link_count // group_count
    row_ints, row_energy = (
        lax.all_gather(orbital_ints, "col", axis=0, tiled=True),
        lax.all_gather(occ_energy.astype(jnp.bfloat16), "col", axis=0, tiled=True).astype(
            occ_energy.dtype
        ),
    )
    col_ints, col_energy = (
        lax.all_gather(orbital_ints, "row", axis=0, tiled=True),
        lax.all_gather(occ_energy.astype(jnp.bfloat16), "row", axis=0, tiled=True).astype(
            occ_energy.dtype
        ),
    )
    block_width = math.gcd(pair_count, 128)
    blocks = pair_count // block_width

    def kernel_block(indices):
        first_ints = jnp.take(row_ints, indices[0], axis=0)
        second_ints = jnp.take(col_ints, indices[1], axis=0)
        return jnp.einsum(
            "pax,pbx->abp", first_ints, second_ints, preferred_element_type=jnp.float32
        )

    stacked = lax.map(
        kernel_block, (pair_row.reshape(blocks, block_width), pair_col.reshape(blocks, block_width))
    )
    partial_kernel = jnp.transpose(stacked, (1, 2, 0, 3)).reshape(tile_size, tile_size, pair_count)
    denominator = (
        virt_energy[:, None, :]
        + virt_energy[None, :, :]
        - (row_energy[pair_row] + col_energy[pair_col])[None, None, :]
    )
    owners = partner_owner[0].T.reshape(-1)
    owner_slots = partner_slot[0].T.reshape(-1)
    onehot = (owners[:, None] == jnp.arange(group_count, dtype=jnp.int32)[None, :]).astype(
        jnp.int32
    )
    position = jnp.sum((jnp.cumsum(onehot, axis=0) - 1) * onehot, axis=1)
    target = owners * capacity + position
    requests = jnp.zeros((group_count * capacity,), jnp.int32).at[target].set(owner_slots)
    incoming = lax.all_to_all(requests, ("row", "col"), split_axis=0, concat_axis=0, tiled=True)
    kernel = lax.psum(partial_kernel.astype(jnp.bfloat16), "fit").astype(jnp.float32)
    current = amplitudes
    residual = amplitudes
    for turn_index in range(ITERS):
        sent_tiles = current.astype(jnp.bfloat16)
        outgoing = jnp.take(sent_tiles, incoming, axis=2)
        returned = lax.all_to_all(outgoing, ("row", "col"), split_axis=2, concat_axis=2, tiled=True)
        coupled_tiles = jnp.take(returned, target, axis=2).reshape(
            tile_size, tile_size, link_count, pair_count
        )
        half_product = jnp.einsum(
            "abcp,bdcp->adcp", intersections, coupled_tiles, preferred_element_type=jnp.float32
        ).astype(jnp.bfloat16)
        coupled = jnp.einsum(
            "adcp,edcp->aecp", half_product, intersections, preferred_element_type=jnp.float32
        )
        coupling = jnp.sum(coupled * coupling_fock[None, None, :, :], axis=2)
        residual = (
            kernel
            + denominator * current
            - lax.psum(coupling.astype(jnp.bfloat16), "fit").astype(jnp.float32)
        )
        current = current - residual / denominator
    return (current, residual)


def solution(mesh):
    placed = (
        P(("row", "col"), None, "fit"),
        P(("row", "col")),
        P(("row", "col")),
        P(("row", "col")),
        P(None, ("row", "col")),
        P(None, None, ("row", "col")),
        P(None, None, "fit", ("row", "col")),
        P("fit", ("row", "col")),
        P("fit", ("row", "col"), None),
        P("fit", ("row", "col"), None),
    )
    return jax.shard_map(
        on_device,
        mesh=mesh,
        in_specs=placed,
        out_specs=(P(None, None, ("row", "col")), P(None, None, ("row", "col"))),
        check_vma=False,
    )
```

profile of v0, /device:TPU:0, one launch (start us, length us, event | category | flops | bytes accessed | tf_op | source)
XLA Modules:
  0.0 474.3 jit_solution(11859671098147663986)
XLA Ops:
  7.2 0.7 broadcast_multiply_fusion
  7.8 0.7 fusion.25
  8.5 1.1 reduce-window.6
  9.9 0.8 fusion.24
  10.7 3.2 scatter_custom_fusion
  13.9 7.3 %all-to-all-start = ((s32[8,128,1]{1,2,0:T(1,128)}), s32[8,128,1]{1,2,0:T(1,128)S(1)}, u32[]{:S(2)}, u32[]{:S(2)}) async-start(s32[8,128,1]{1,2,0:T(1,128)} %bitcast.29), calls=%async_computation | async-start | bytes 8192 | tf_op jit(solution)/shard_map/all_to_all | solution.py:68
  21.2 1.2 convert_element_type.66
  22.4 1.5 copy.61
  23.8 3.7 all-to-all-done
  27.6 11.1 %gather_fusion.2 = bf16[1024,40,40]{2,1,0:T(8,128)(2,1)} fusion(bf16[40,40,128]{1,0,2:T(8,128)(2,1)S(1)} %copy.61, s32[1024]{0:T(1024)S(1)} %fusion.26), kind=kCustom, calls=%fused_computation.clone | custom fusion | bytes 6557696 | tf_op jit(solution)/shard_map/jit(_take)/gather | solution.py:74
  38.7 11.5 %fusion.35 = bf16[1024,40,40]{2,1,0:T(8,128)(2,1)} fusion(bf16[1024,40,40]{2,1,0:T(8,128)(2,1)} %gather_fusion.2, pred[1024]{0:T(1024)(128)(4,1)S(1)} %compare_and_fusion), kind=kLoop, calls=%fused_computation.75 | loop fusion | flops 1638400 | bytes 6554624
  50.2 17.7 %reshape.213 = bf16[8,2,102400]{2,1,0:T(2,128)(2,1)} reshape(bf16[1024,40,40]{2,1,0:T(8,128)(2,1)} %fusion.35) | data formatting | bytes 6553600
  67.9 4.6 all-to-all-start.1
  72.6 0.6 dynamic-slice.3
  73.1 0.6 dynamic-slice.2
  75.1 0.2 dynamic-update-slice.1
  75.5 8.7 %all-reduce.1 = bf16[4]{0:T(256)(128)(2,1)S(1)} all-reduce(bf16[4]{0:T(256)(128)(2,1)S(1)} %dynamic-update-slice.1), channel_id=1, replica_groups=mesh['row'=2,'col'=4,'fit'=4] {'row'}, use_global_device_ids=true, to_apply=%add.1 | all-reduce | flops 4 | bytes 16
  84.2 48.3 %all-reduce = bf16[8]{0:T(256)(128)(2,1)S(1)} all-reduce(bf16[8]{0:T(256)(128)(2,1)S(1)} %dynamic-update-slice), channel_id=1, replica_groups=mesh['row'=2,'col'=4,'fit'=4] {'col'}, use_global_device_ids=true, to_apply=%add | all-reduce | flops 8 | bytes 32
  132.5 4.7 copy.63
  137.2 28.7 %all_gather.13 = bf16[8,40,640]{2,1,0:T(8,128)(2,1)S(1)} all-gather(bf16[2,40,640]{2,1,0:T(8,128)(2,1)S(1)} %copy-done.5), channel_id=1, replica_groups=mesh['row'=2,'col'=4,'fit'=4] {'col'}, dimensions={0}, use_global_device_ids=true | all-gather | bytes 512000 | tf_op jit(solution)/shard_map/all_gather | solution.py:30
  166.0 4.1 gather_fusion.1
  170.1 5.5 %all_gather.12 = bf16[4,40,640]{2,1,0:T(8,128)(2,1)S(1)} all-gather(bf16[2,40,640]{2,1,0:T(8,128)(2,1)S(1)} %copy-done.5), channel_id=1, replica_groups=mesh['row'=2,'col'=4,'fit'=4] {'row'}, dimensions={0}, use_global_device_ids=true | all-gather | bytes 307200 | tf_op jit(solution)/shard_map/all_gather | solution.py:36
  175.6 4.1 gather_fusion
  179.8 7.2 %fusion = bf16[128,40,40]{2,1,0:T(8,128)(2,1)S(1)} fusion(bf16[128,40,640]{2,1,0:T(8,128)(2,1)} %gather_fusion.1, bf16[128,40,640]{2,1,0:T(8,128)(2,1)} %gather_fusion, pred[128]{0:T(512)(128)(4,1)S(1)} %get-tuple-element.46, pred[128]{0:T(512)(128)(4,1)S(1)} %get-tuple-element.47), kind=kOutput, calls=%fused_computation.11 | convolution fusion | flops 268697600 | bytes 13517056 | tf_op jit(solution)/shard_map/while/body/eval_jaxpr/pax,pbx->abp/dot_general | solution.py:47
  187.0 1.9 copy.59
  188.9 18.7 %reshape.214 = bf16[1024,40,40]{2,1,0:T(8,128)(2,1)} reshape(bf16[8,2,102400]{2,1,0:T(2,128)(2,1)} %all-to-all-done.1) | data formatting | bytes 6553600
  207.6 7.9 %gather_fusion.3 = bf16[512,40,40]{2,1,0:T(8,128)(2,1)} fusion(bf16[40,40,1024]{1,0,2:T(8,128)(2,1)} %bitcast.87, s32[1024]{0:T(1024)S(1)} %pad_clamp_fusion), kind=kCustom, calls=%fused_computation.1.clone | custom fusion | bytes 3278848 | tf_op jit(solution)/shard_map/jit(_take)/gather | solution.py:76
  215.5 6.7 %broadcast_select_fusion.1 = bf16[512,40,40]{2,1,0:T(8,128)(2,1)} fusion(bf16[512,40,40]{2,1,0:T(8,128)(2,1)} %gather_fusion.3, pred[512]{0:T(512)(128)(4,1)S(1)} %get-tuple-element.32), kind=kLoop, calls=%fused_computation.23 | loop fusion | flops 819200 | bytes 3277312 | tf_op jit(solution)/shard_map/jit(_take)/select_n | solution.py:76
  222.2 9.7 %multiply_reduce_fusion.1 = bf16[128,40,40]{2,1,0:T(8,128)(2,1)S(1)} fusion(f32[4,128]{1,0:T(4,128)S(1)} %copy-done.10, bf16[40,40,4,128]{1,0,3,2:T(8,128)(2,1)} %copy.63, bf16[40,40,4,128]{1,0,3,2:T(8,128)(2,1)} %bitcast.89), kind=kOutput, calls=%fused_computation.10 | convolution fusion | flops 133324800 | bytes 3688448 | tf_op jit(solution)/shard_map/adcp,edcp->aecp/dot_general | solution.py:82
  231.8 1.7 copy.66
  233.6 0.3 all-reduce.6.cloned.1.call-start
  233.8 0.7 fusion.34
  234.5 0.7 fusion.33
  235.2 7.7 %fusion.29 = f32[128]{0:T(128)S(1)} fusion(f32[]{:T(128)} %bitcast.11, f32[]{:T(128)} %bitcast.12, f32[]{:T(128)} %bitcast.13, f32[]{:T(128)} %bitcast.14, f32[]{:T(128)} %bitcast.2, f32[]{:T(128)} %bitcast.3, f32[]{:T(128)} %bitcast.4, f32[]{:T(128)} %bitcast.5, f32[]{:T(128)} %bitcast.6, f32[]{:T(128)} %bitcast.7, f32[]{:T(128)} %bitcast.8, f32[]{:T(128)} %bitcast.9, ...), kind=kLoop, calls=%fused_computation.70 | loop fusion | flops 3456 | bytes 1584 | tf_op jit(solution)/shard_map/add | solution.py:58
  242.9 26.0 %all-reduce.8.cloned.1.call-done = (bf16[40,40,128]{2,1,0:T(8,128)(2,1)}, bf16[40,40,128]{2,1,0:T(8,128)(2,1)}) async-done(((bf16[40,40,128]{2,1,0:T(8,128)(2,1)}, bf16[40,40,128]{2,1,0:T(8,128)(2,1)}), (bf16[40,40,128]{2,1,0:T(8,128)(2,1)}, bf16[40,40,128]{2,1,0:T(8,128)(2,1)})) %all-reduce.8.cloned.1.call-update) | async-done | bytes 819216 | tf_op jit(solution)/shard_map/psum | solution.py:69
  268.9 1.4 fusion.31
  270.3 1.5 copy.67
  271.8 11.1 %gather_fusion.4 = bf16[1024,40,40]{2,1,0:T(8,128)(2,1)} fusion(bf16[40,40,128]{1,0,2:T(8,128)(2,1)S(1)} %copy.67, s32[1024]{0:T(1024)S(1)} %fusion.26), kind=kCustom, calls=%fused_computation.2.clone | custom fusion | bytes 6557696 | tf_op jit(solution)/shard_map/jit(_take)/gather | solution.py:74
  282.9 11.5 %fusion.36 = bf16[1024,40,40]{2,1,0:T(8,128)(2,1)} fusion(bf16[1024,40,40]{2,1,0:T(8,128)(2,1)} %gather_fusion.4, pred[1024]{0:T(1024)(128)(4,1)S(1)} %compare_and_fusion), kind=kLoop, calls=%fused_computation.76 | loop fusion | flops 1638400 | bytes 6554624
  294.4 16.9 %reshape.215 = bf16[8,2,102400]{2,1,0:T(2,128)(2,1)S(1)} reshape(bf16[1024,40,40]{2,1,0:T(8,128)(2,1)} %fusion.36) | data formatting | bytes 6553600
  311.3 78.9 %all_to_all.22 = bf16[8,2,102400]{2,1,0:T(2,128)(2,1)} all-to-all(bf16[8,2,102400]{2,1,0:T(2,128)(2,1)S(1)} %reshape.215), channel_id=1, replica_groups=mesh['row'=2,'col'=4,'fit'=4] {'row','col'}, dimensions={0} | all-to-all | bytes 6553600 | tf_op jit(solution)/shard_map/all_to_all | solution.py:75
  390.2 18.7 %reshape.216 = bf16[1024,40,40]{2,1,0:T(8,128)(2,1)} reshape(bf16[8,2,102400]{2,1,0:T(2,128)(2,1)} %all_to_all.22) | data formatting | bytes 6553600
  408.9 7.9 %gather_fusion.5 = bf16[512,40,40]{2,1,0:T(8,128)(2,1)} fusion(bf16[40,40,1024]{1,0,2:T(8,128)(2,1)} %bitcast.86, s32[1024]{0:T(1024)S(1)} %pad_clamp_fusion), kind=kCustom, calls=%fused_computation.3.clone | custom fusion | bytes 3278848 | tf_op jit(solution)/shard_map/jit(_take)/gather | solution.py:76
  416.8 6.7 %broadcast_select_fusion = bf16[512,40,40]{2,1,0:T(8,128)(2,1)} fusion(bf16[512,40,40]{2,1,0:T(8,128)(2,1)} %gather_fusion.5, pred[512]{0:T(512)(128)(4,1)S(1)} %get-tuple-element.32), kind=kLoop, calls=%fused_computation.22 | loop fusion | flops 819200 | bytes 3277312 | tf_op jit(solution)/shard_map/jit(_take)/select_n | solution.py:76
  423.5 9.7 %multiply_reduce_fusion = bf16[128,40,40]{2,1,0:T(8,128)(2,1)S(1)} fusion(f32[4,128]{1,0:T(4,128)S(1)} %copy-done.10, bf16[40,40,4,128]{1,0,3,2:T(8,128)(2,1)} %copy.63, bf16[40,40,4,128]{1,0,3,2:T(8,128)(2,1)} %bitcast.88), kind=kOutput, calls=%fused_computation.9 | convolution fusion | flops 133324800 | bytes 3688448 | tf_op jit(solution)/shard_map/adcp,edcp->aecp/dot_general | solution.py:82
  433.2 1.7 copy.72
  434.9 29.9 %all-reduce.6.cloned.1.call-done = bf16[40,40,128]{2,1,0:T(8,128)(2,1)} async-done(((bf16[40,40,128]{2,1,0:T(8,128)(2,1)}), bf16[40,40,128]{2,1,0:T(8,128)(2,1)}) %all-reduce.6.cloned.1.call-update) | async-done | bytes 409616 | tf_op jit(solution)/shard_map/psum | solution.py:89
  464.8 2.6 divide_subtract_fusion
  (49 shorter events, 0.7 us)
Async XLA Ops:
  13.9 13.7 %all-to-all-start = ((s32[8,128,1]{1,2,0:T(1,128)}), s32[8,128,1]{1,2,0:T(1,128)S(1)}, u32[]{:S(2)}, u32[]{:S(2)}) async-start(s32[8,128,1]{1,2,0:T(1,128)} %bitcast.29), calls=%async_computation | async-start | bytes 8192 | tf_op jit(solution)/shard_map/all_to_all | solution.py:68
  67.9 4.7 copy-start.13
  67.9 5.3 %copy-start.12 = (u32[32]{0:T(128)S(1)}, u32[32]{0:T(128)}, u32[]{:S(2)}) copy-start(u32[32]{0:T(128)} %constant.103) | copy-start | bytes 388
  67.9 7.2 %copy-start.11 = (f32[2]{0:T(128)S(1)}, f32[2]{0:T(128)}, u32[]{:S(2)}) copy-start(f32[2]{0:T(128)} %param.15) | copy-start | bytes 28
  67.9 64.6 %copy-start.2 = (bf16[40,40,4,128]{3,2,1,0:T(4,128)(2,1)S(1)}, bf16[40,40,4,128]{3,2,1,0:T(4,128)(2,1)}, u32[]{:S(2)}) copy-start(bf16[40,40,4,128]{3,2,1,0:T(4,128)(2,1)} %param.20) | copy-start | bytes 4915204
  67.9 69.4 %copy-start.9 = (s32[128]{0:T(128)S(1)}, s32[128]{0:T(128)}, u32[]{:S(2)}) copy-start(s32[128]{0:T(128)} %param.16) | copy-start | bytes 1540
  67.9 69.4 %copy-start.5 = (bf16[2,40,640]{2,1,0:T(8,128)(2,1)S(1)}, bf16[2,40,640]{2,1,0:T(8,128)(2,1)}, u32[]{:S(2)}) copy-start(bf16[2,40,640]{2,1,0:T(8,128)(2,1)} %param.14) | copy-start | bytes 307204
  67.9 121.0 %all-to-all-start.1 = ((bf16[8,2,102400]{2,1,0:T(2,128)(2,1)}), bf16[8,2,102400]{2,1,0:T(2,128)(2,1)}, u32[]{:S(2)}, u32[]{:S(2)}) async-start(bf16[8,2,102400]{2,1,0:T(2,128)(2,1)} %reshape.213), calls=%async_computation.1 | async-start | bytes 6553600 | tf_op jit(solution)/shard_map/all_to_all | solution.py:75
  72.5 196.4 %all-reduce.8.cloned.1.call-start = ((), (), s32[]{:S(2)}) async-start(), calls=%async_computation.4 | async-start | bytes 1638400 | tf_op jit(solution)/shard_map/psum | solution.py:69
  166.0 9.6 %copy-start.8 = (s32[128]{0:T(128)S(1)}, s32[128]{0:T(128)}, u32[]{:S(2)}) copy-start(s32[128]{0:T(128)} %param.17) | copy-start | bytes 1540
  179.7 9.1 %copy-start.7 = (s32[1,128,4]{1,2,0:T(4,128)S(1)}, s32[1,128,4]{1,2,0:T(4,128)}, u32[]{:S(2)}) copy-start(s32[1,128,4]{1,2,0:T(4,128)} %param.22) | copy-start | bytes 6148
  215.5 6.7 %copy-start.10 = (f32[4,128]{1,0:T(4,128)S(1)}, f32[4,128]{1,0:T(4,128)}, u32[]{:S(2)}) copy-start(f32[4,128]{1,0:T(4,128)} %param.21) | copy-start | bytes 6148
  222.2 46.8 %copy-start = (f32[40,40,128]{2,1,0:T(8,128)S(1)}, f32[40,40,128]{2,1,0:T(8,128)}, u32[]{:S(2)}) copy-start(f32[40,40,128]{2,1,0:T(8,128)} %param.19) | copy-start | bytes 2457604
  222.2 46.8 %copy-start.6 = (f32[40,128]{1,0:T(8,128)S(1)}, f32[40,128]{1,0:T(8,128)}, u32[]{:S(2)}) copy-start(f32[40,128]{1,0:T(8,128)} %param.18) | copy-start | bytes 61444
  233.6 231.3 %all-reduce.6.cloned.1.call-start = ((), (), s32[]{:S(2)}) async-start(), calls=%async_computation.3 | async-start | bytes 819200 | tf_op jit(solution)/shard_map/psum | solution.py:89
  423.5 41.4 %copy-start.1 = (f32[40,40,128]{2,1,0:T(8,128)S(1)}, f32[40,40,128]{2,1,0:T(8,128)}, u32[]{:S(2)}) copy-start(f32[40,40,128]{2,1,0:T(8,128)} %param.19) | copy-start | bytes 2457604
  423.5 41.4 %copy-start.3 = (bf16[40,40,128]{2,1,0:T(8,128)(2,1)S(1)}, bf16[40,40,128]{2,1,0:T(8,128)(2,1)}, u32[]{:S(2)}) copy-start(bf16[40,40,128]{2,1,0:T(8,128)(2,1)} %get-tuple-element.28) | copy-start | bytes 1228804
  423.5 41.4 %copy-start.4 = (bf16[40,40,128]{2,1,0:T(8,128)(2,1)S(1)}, bf16[40,40,128]{2,1,0:T(8,128)(2,1)}, u32[]{:S(2)}) copy-start(bf16[40,40,128]{2,1,0:T(8,128)(2,1)} %get-tuple-element.29) | copy-start | bytes 1228804
Sparse Core Ops, SparseCore 0:
  233.7 35.1 all-reduce.7
  435.0 29.7 all-reduce.5
where the time goes:
time: 475 us; the launch traced here: 474 us
  blocking collectives  170 us (36%)
  local copies, waits for them, and re-layouts  138 us (29%)
  waiting for transfers between devices  59.7 us (13%)
  other arithmetic  52.6 us (11%)
  matrix products  26.6 us (6%)
  between operations  15.5 us (3%)
  starting transfers between devices  12.2 us (3%)
    all_to_all x1, blocking collectives, on_device(): lax.all_to_all(outgoing, ('row', 'col'), split_axis=2, concat_axis=2, til...  78.9 us
    unnamed x39, local copies, waits for them, and re-layouts  78.5 us
    unnamed x2, blocking collectives  57 us
    psum x1, waiting for transfers between devices, on_device(): lax.psum(coupling.astype(jnp.bfloat16), 'fit').astype(jnp.float32)  29.9 us
    all_gather x1, blocking collectives, on_device(): lax.all_gather(orbital_ints, 'col', axis=0, tiled=True)  28.7 us
    psum x1, waiting for transfers between devices, on_device(): lax.psum(partial_kernel.astype(jnp.bfloat16), 'fit').astype(jnp.float32)  26 us
    unnamed x2, other arithmetic  22.9 us
    gather x2, local copies, waits for them, and re-layouts, on_device(): outgoing = jnp.take(sent_tiles, incoming, axis=2)  22.2 us
  transfers between devices with their start and end apart: 4, of which 3 were waited for; matrix products, arithmetic and copies ran while one was open for 7% of the time, Pallas kernels for 0%

commit v1 on v0

--- a/solution.py
+++ b/solution.py
@@ -86,7 +86,9 @@
         residual = (
             kernel
             + denominator * current
-            - lax.psum(coupling.astype(jnp.bfloat16), "fit").astype(jnp.float32)
+            - jnp.sum(lax.all_gather(coupling.astype(jnp.bfloat16), "fit"), axis=0).astype(
+                jnp.float32
+            )
         )
         current = current - residual / denominator
     return (current, residual)

time: 475 us -> 454 us (0.956)
  blocking collectives: 170 us -> 113 us
  waiting for transfers between devices: 59.7 us -> 93.1 us
    all_to_all x1, waiting for transfers between devices: 0.01 us -> 66.4 us  [on_device(): lax.all_to_all(outgoing, ('row', 'col'), split_axis=2, concat_axis=2, til...]
    unnamed x2, blocking collectives: 57 us -> 14.1 us
    psum x1 -> x0, waiting for transfers between devices: 29.9 us -> none  [on_device(): lax.psum(coupling.astype(jnp.bfloat16), 'fit').astype(jnp.float32)]
    psum x1, waiting for transfers between devices: 26 us -> 5.43 us  [on_device(): lax.psum(partial_kernel.astype(jnp.bfloat16), 'fit').astype(jnp.float32)]
    all_gather x0 -> x2, waiting for transfers between devices: none -> 17.5 us  [on_device(): lax.all_gather(coupling.astype(jnp.bfloat16), 'fit')]
    all_gather x1, blocking collectives: 28.7 us -> 14.3 us  [on_device(): lax.all_gather(orbital_ints, 'col', axis=0, tiled=True)]
  transfers between devices with their start and end apart: 4 -> 5, of which waited for: 3 -> 4; matrix products, arithmetic and copies ran while one was open for 7% -> 9% of each run, Pallas kernels for 0% -> 0%
where the time goes in v1:
time: 454 us; the launch traced here: 453 us
  local copies, waits for them, and re-layouts  138 us (30%)
  blocking collectives  113 us (25%)
  waiting for transfers between devices  93.1 us (21%)
  other arithmetic  54.8 us (12%)
  matrix products  26.7 us (6%)
  between operations  15.3 us (3%)
  starting transfers between devices  11.4 us (3%)
    unnamed x39, local copies, waits for them, and re-layouts  79.2 us
    all_to_all x1, blocking collectives, on_device(): lax.all_to_all(outgoing, ('row', 'col'), split_axis=2, concat_axis=2, til...  79 us
    all_to_all x1, waiting for transfers between devices, on_device(): lax.all_to_all(outgoing, ('row', 'col'), split_axis=2, concat_axis=2, til...  66.4 us
    unnamed x2, other arithmetic  22.8 us
    gather x2, local copies, waits for them, and re-layouts, on_device(): outgoing = jnp.take(sent_tiles, incoming, axis=2)  22.2 us
    dot_general x2, matrix products, on_device(): jnp.einsum('adcp,edcp->aecp', half_product, intersections, preferred_elem...  19.4 us
    all_gather x2, waiting for transfers between devices, on_device(): lax.all_gather(coupling.astype(jnp.bfloat16), 'fit')  17.5 us
    gather x2, local copies, waits for them, and re-layouts, on_device(): jnp.take(returned, target, axis=2)  15.8 us
  transfers between devices with their start and end apart: 5, of which 4 were waited for; matrix products, arithmetic and copies ran while one was open for 9% of the time, Pallas kernels for 0%

profile of v1, /device:TPU:0, one launch (start us, length us, event | category | flops | bytes accessed | tf_op | source)
XLA Modules:
  0.0 452.7 jit_solution(7398432759675700407)
XLA Ops:
  7.2 0.7 broadcast_multiply_fusion
  7.8 0.7 fusion.25
  8.5 1.1 reduce-window.6
  9.9 0.8 fusion.24
  10.7 3.2 scatter_custom_fusion
  13.9 7.3 %all-to-all-start = ((s32[8,128,1]{1,2,0:T(1,128)}), s32[8,128,1]{1,2,0:T(1,128)S(1)}, u32[]{:S(2)}, u32[]{:S(2)}) async-start(s32[8,128,1]{1,2,0:T(1,128)} %bitcast.29), calls=%async_computation | async-start | bytes 8192 | tf_op jit(solution)/shard_map/all_to_all | solution.py:68
  21.2 1.2 convert_element_type.90
  22.4 1.5 copy.95
  23.8 3.7 all-to-all-done
  27.6 11.1 %gather_fusion.2 = bf16[1024,40,40]{2,1,0:T(8,128)(2,1)} fusion(bf16[40,40,128]{1,0,2:T(8,128)(2,1)S(1)} %copy.95, s32[1024]{0:T(1024)S(1)} %fusion.26), kind=kCustom, calls=%fused_computation.clone | custom fusion | bytes 6557696 | tf_op jit(solution)/shard_map/jit(_take)/gather | solution.py:74
  38.7 11.4 %fusion.35 = bf16[1024,40,40]{2,1,0:T(8,128)(2,1)} fusion(bf16[1024,40,40]{2,1,0:T(8,128)(2,1)} %gather_fusion.2, pred[1024]{0:T(1024)(128)(4,1)S(1)} %compare_and_fusion), kind=kLoop, calls=%fused_computation.75 | loop fusion | flops 1638400 | bytes 6554624
  50.1 17.7 %reshape.231 = bf16[8,2,102400]{2,1,0:T(2,128)(2,1)} reshape(bf16[1024,40,40]{2,1,0:T(8,128)(2,1)} %fusion.35) | data formatting | bytes 6553600
  67.9 3.8 all-to-all-start.1
  71.9 6.5 %copy.97 = bf16[40,40,4,128]{1,0,3,2:T(8,128)(2,1)} copy(bf16[40,40,4,128]{3,2,1,0:T(4,128)(2,1)} %param.20) | data formatting | bytes 3276800 | tf_op args[6]
  78.4 66.4 %all-to-all-done.1 = bf16[8,2,102400]{2,1,0:T(2,128)(2,1)S(1)} async-done(((bf16[8,2,102400]{2,1,0:T(2,128)(2,1)}), bf16[8,2,102400]{2,1,0:T(2,128)(2,1)S(1)}, u32[]{:S(2)}, u32[]{:S(2)}) %all-to-all-start.1) | async-done | bytes 3276832 | tf_op jit(solution)/shard_map/all_to_all | solution.py:75
  144.8 17.6 %reshape.232 = bf16[1024,40,40]{2,1,0:T(8,128)(2,1)} reshape(bf16[8,2,102400]{2,1,0:T(2,128)(2,1)S(1)} %all-to-all-done.1) | data formatting | bytes 6553600
  162.4 7.9 %gather_fusion.3 = bf16[512,40,40]{2,1,0:T(8,128)(2,1)} fusion(bf16[40,40,1024]{1,0,2:T(8,128)(2,1)} %bitcast.89, s32[1024]{0:T(1024)S(1)} %pad_clamp_fusion), kind=kCustom, calls=%fused_computation.1.clone | custom fusion | bytes 3278848 | tf_op jit(solution)/shard_map/jit(_take)/gather | solution.py:76
  170.3 6.7 %broadcast_select_fusion.1 = bf16[512,40,40]{2,1,0:T(8,128)(2,1)} fusion(bf16[512,40,40]{2,1,0:T(8,128)(2,1)} %gather_fusion.3, pred[512]{0:T(512)(128)(4,1)S(1)} %get-tuple-element.34), kind=kLoop, calls=%fused_computation.23 | loop fusion | flops 819200 | bytes 3277312 | tf_op jit(solution)/shard_map/jit(_take)/select_n | solution.py:76
  177.1 9.7 %multiply_reduce_fusion.1 = bf16[128,40,40]{2,1,0:T(8,128)(2,1)S(1)} fusion(f32[4,128]{1,0:T(4,128)S(1)} %copy-done.10, bf16[40,40,4,128]{1,0,3,2:T(8,128)(2,1)} %copy.97, bf16[40,40,4,128]{1,0,3,2:T(8,128)(2,1)} %bitcast.91), kind=kOutput, calls=%fused_computation.10 | convolution fusion | flops 133324800 | bytes 3688448 | tf_op jit(solution)/shard_map/adcp,edcp->aecp/dot_general | solution.py:82
  186.7 1.7 copy.100
  189.1 0.6 dynamic-slice.2
  191.1 14.3 %all_gather.21 = bf16[8,40,640]{2,1,0:T(8,128)(2,1)S(1)} all-gather(bf16[2,40,640]{2,1,0:T(8,128)(2,1)S(1)} %copy-done.5), channel_id=1, replica_groups=mesh['row'=2,'col'=4,'fit'=4] {'col'}, dimensions={0}, use_global_device_ids=true | all-gather | bytes 512000 | tf_op jit(solution)/shard_map/all_gather | solution.py:30
  205.4 4.2 gather_fusion.1
  209.6 5.5 %all_gather.20 = bf16[4,40,640]{2,1,0:T(8,128)(2,1)S(1)} all-gather(bf16[2,40,640]{2,1,0:T(8,128)(2,1)S(1)} %copy-done.5), channel_id=1, replica_groups=mesh['row'=2,'col'=4,'fit'=4] {'row'}, dimensions={0}, use_global_device_ids=true | all-gather | bytes 307200 | tf_op jit(solution)/shard_map/all_gather | solution.py:36
  215.2 4.1 gather_fusion
  219.3 7.3 %fusion = bf16[128,40,40]{2,1,0:T(8,128)(2,1)S(1)} fusion(bf16[128,40,640]{2,1,0:T(8,128)(2,1)} %gather_fusion.1, bf16[128,40,640]{2,1,0:T(8,128)(2,1)} %gather_fusion, pred[128]{0:T(512)(128)(4,1)S(1)} %get-tuple-element.48, pred[128]{0:T(512)(128)(4,1)S(1)} %get-tuple-element.49), kind=kOutput, calls=%fused_computation.11 | convolution fusion | flops 268697600 | bytes 13517056 | tf_op jit(solution)/shard_map/while/body/eval_jaxpr/pax,pbx->abp/dot_general | solution.py:47
  226.6 1.9 copy.93
  228.9 4.9 %all-reduce.1 = bf16[4]{0:T(256)(128)(2,1)S(1)} all-reduce(bf16[4]{0:T(256)(128)(2,1)S(1)} %dynamic-update-slice.1), channel_id=1, replica_groups=mesh['row'=2,'col'=4,'fit'=4] {'row'}, use_global_device_ids=true, to_apply=%add.1 | all-reduce | flops 4 | bytes 16
  233.8 9.1 %all-reduce = bf16[8]{0:T(256)(128)(2,1)S(1)} all-reduce(bf16[8]{0:T(256)(128)(2,1)S(1)} %dynamic-update-slice), channel_id=1, replica_groups=mesh['row'=2,'col'=4,'fit'=4] {'col'}, use_global_device_ids=true, to_apply=%add | all-reduce | flops 8 | bytes 32
  243.0 0.7 fusion.34
  243.6 0.7 fusion.33
  244.3 7.6 %fusion.29 = f32[128]{0:T(128)S(1)} fusion(f32[]{:T(128)} %bitcast.11, f32[]{:T(128)} %bitcast.12, f32[]{:T(128)} %bitcast.13, f32[]{:T(128)} %bitcast.14, f32[]{:T(128)} %bitcast.2, f32[]{:T(128)} %bitcast.3, f32[]{:T(128)} %bitcast.4, f32[]{:T(128)} %bitcast.5, f32[]{:T(128)} %bitcast.6, f32[]{:T(128)} %bitcast.7, f32[]{:T(128)} %bitcast.8, f32[]{:T(128)} %bitcast.9, ...), kind=kLoop, calls=%fused_computation.70 | loop fusion | flops 3456 | bytes 1584 | tf_op jit(solution)/shard_map/add | solution.py:58
  251.9 1.8 reduce_sum.56
  253.8 5.4 %all-reduce.4.cloned.1.call-done = bf16[40,40,128]{2,1,0:T(8,128)(2,1)} async-done(((bf16[40,40,128]{2,1,0:T(8,128)(2,1)}), bf16[40,40,128]{2,1,0:T(8,128)(2,1)}) %all-reduce.4.cloned.1.call-update) | async-done | bytes 409616 | tf_op jit(solution)/shard_map/psum | solution.py:69
  259.2 1.3 fusion.31
  260.5 1.5 copy.101
  262.0 11.1 %gather_fusion.4 = bf16[1024,40,40]{2,1,0:T(8,128)(2,1)} fusion(bf16[40,40,128]{1,0,2:T(8,128)(2,1)S(1)} %copy.101, s32[1024]{0:T(1024)S(1)} %fusion.26), kind=kCustom, calls=%fused_computation.2.clone | custom fusion | bytes 6557696 | tf_op jit(solution)/shard_map/jit(_take)/gather | solution.py:74
  273.1 11.4 %fusion.36 = bf16[1024,40,40]{2,1,0:T(8,128)(2,1)} fusion(bf16[1024,40,40]{2,1,0:T(8,128)(2,1)} %gather_fusion.4, pred[1024]{0:T(1024)(128)(4,1)S(1)} %compare_and_fusion), kind=kLoop, calls=%fused_computation.76 | loop fusion | flops 1638400 | bytes 6554624
  284.5 16.9 %reshape.233 = bf16[8,2,102400]{2,1,0:T(2,128)(2,1)S(1)} reshape(bf16[1024,40,40]{2,1,0:T(8,128)(2,1)} %fusion.36) | data formatting | bytes 6553600
  301.4 79.0 %all_to_all.22 = bf16[8,2,102400]{2,1,0:T(2,128)(2,1)} all-to-all(bf16[8,2,102400]{2,1,0:T(2,128)(2,1)S(1)} %reshape.233), channel_id=1, replica_groups=mesh['row'=2,'col'=4,'fit'=4] {'row','col'}, dimensions={0} | all-to-all | bytes 6553600 | tf_op jit(solution)/shard_map/all_to_all | solution.py:75
  380.5 18.7 %reshape.234 = bf16[1024,40,40]{2,1,0:T(8,128)(2,1)} reshape(bf16[8,2,102400]{2,1,0:T(2,128)(2,1)} %all_to_all.22) | data formatting | bytes 6553600
  399.2 7.9 %gather_fusion.5 = bf16[512,40,40]{2,1,0:T(8,128)(2,1)} fusion(bf16[40,40,1024]{1,0,2:T(8,128)(2,1)} %bitcast.88, s32[1024]{0:T(1024)S(1)} %pad_clamp_fusion), kind=kCustom, calls=%fused_computation.3.clone | custom fusion | bytes 3278848 | tf_op jit(solution)/shard_map/jit(_take)/gather | solution.py:76
  407.1 6.6 %broadcast_select_fusion = bf16[512,40,40]{2,1,0:T(8,128)(2,1)} fusion(bf16[512,40,40]{2,1,0:T(8,128)(2,1)} %gather_fusion.5, pred[512]{0:T(512)(128)(4,1)S(1)} %get-tuple-element.34), kind=kLoop, calls=%fused_computation.22 | loop fusion | flops 819200 | bytes 3277312 | tf_op jit(solution)/shard_map/jit(_take)/select_n | solution.py:76
  413.7 9.7 %multiply_reduce_fusion = bf16[128,40,40]{2,1,0:T(8,128)(2,1)S(1)} fusion(f32[4,128]{1,0:T(4,128)S(1)} %copy-done.10, bf16[40,40,4,128]{1,0,3,2:T(8,128)(2,1)} %copy.97, bf16[40,40,4,128]{1,0,3,2:T(8,128)(2,1)} %bitcast.90), kind=kOutput, calls=%fused_computation.9 | convolution fusion | flops 133324800 | bytes 3688448 | tf_op jit(solution)/shard_map/adcp,edcp->aecp/dot_general | solution.py:82
  423.5 1.7 copy.106
  425.2 17.4 %all-gather.7.cloned.1.call-done = bf16[160,40,128]{2,1,0:T(8,128)(2,1)} async-done(((bf16[40,40,128]{2,1,0:T(8,128)(2,1)}), bf16[160,40,128]{2,1,0:T(8,128)(2,1)}) %all-gather.7.cloned.1.call-update) | async-done | bytes 1638416 | tf_op jit(solution)/shard_map/all_gather | solution.py:89
  442.7 1.8 reduce_sum.58
  444.6 1.6 divide_subtract_fusion
  (54 shorter events, 1.8 us)
Async XLA Ops:
  13.9 13.7 %all-to-all-start = ((s32[8,128,1]{1,2,0:T(1,128)}), s32[8,128,1]{1,2,0:T(1,128)S(1)}, u32[]{:S(2)}, u32[]{:S(2)}) async-start(s32[8,128,1]{1,2,0:T(1,128)} %bitcast.29), calls=%async_computation | async-start | bytes 8192 | tf_op jit(solution)/shard_map/all_to_all | solution.py:68
  67.9 10.5 %copy-start.7 = (s32[1,128,4]{1,2,0:T(4,128)S(1)}, s32[1,128,4]{1,2,0:T(4,128)}, u32[]{:S(2)}) copy-start(s32[1,128,4]{1,2,0:T(4,128)} %param.22) | copy-start | bytes 6148
  67.9 77.0 %all-to-all-start.1 = ((bf16[8,2,102400]{2,1,0:T(2,128)(2,1)}), bf16[8,2,102400]{2,1,0:T(2,128)(2,1)S(1)}, u32[]{:S(2)}, u32[]{:S(2)}) async-start(bf16[8,2,102400]{2,1,0:T(2,128)(2,1)} %reshape.231), calls=%async_computation.1 | async-start | bytes 6553600 | tf_op jit(solution)/shard_map/all_to_all | solution.py:75
  71.7 180.3 %all-gather.5.cloned.1.call-start = ((), (), s32[]{:S(2)}) async-start(), calls=%async_computation.4 | async-start | bytes 2048000 | tf_op jit(solution)/shard_map/all_gather | solution.py:89
  170.3 6.7 %copy-start.10 = (f32[4,128]{1,0:T(4,128)S(1)}, f32[4,128]{1,0:T(4,128)}, u32[]{:S(2)}) copy-start(f32[4,128]{1,0:T(4,128)} %param.21) | copy-start | bytes 6148
  177.0 11.5 %copy-start.13 = (u32[32]{0:T(128)S(1)}, u32[32]{0:T(128)}, u32[]{:S(2)}) copy-start(u32[32]{0:T(128)} %constant.111) | copy-start | bytes 388
  177.0 12.1 %copy-start.12 = (u32[32]{0:T(128)S(1)}, u32[32]{0:T(128)}, u32[]{:S(2)}) copy-start(u32[32]{0:T(128)} %constant.106) | copy-start | bytes 388
  177.0 14.0 %copy-start.11 = (f32[2]{0:T(128)S(1)}, f32[2]{0:T(128)}, u32[]{:S(2)}) copy-start(f32[2]{0:T(128)} %param.15) | copy-start | bytes 28
  177.0 14.0 %copy-start.9 = (s32[128]{0:T(128)S(1)}, s32[128]{0:T(128)}, u32[]{:S(2)}) copy-start(s32[128]{0:T(128)} %param.16) | copy-start | bytes 1540
  177.1 14.0 %copy-start.5 = (bf16[2,40,640]{2,1,0:T(8,128)(2,1)S(1)}, bf16[2,40,640]{2,1,0:T(8,128)(2,1)}, u32[]{:S(2)}) copy-start(bf16[2,40,640]{2,1,0:T(8,128)(2,1)} %param.14) | copy-start | bytes 307204
  188.5 70.7 %all-reduce.4.cloned.1.call-start = ((), (), s32[]{:S(2)}) async-start(), calls=%async_computation.3 | async-start | bytes 819200 | tf_op jit(solution)/shard_map/psum | solution.py:69
  205.4 9.8 %copy-start.8 = (s32[128]{0:T(128)S(1)}, s32[128]{0:T(128)}, u32[]{:S(2)}) copy-start(s32[128]{0:T(128)} %param.17) | copy-start | bytes 1540
  219.2 40.0 %copy-start = (f32[40,40,128]{2,1,0:T(8,128)S(1)}, f32[40,40,128]{2,1,0:T(8,128)}, u32[]{:S(2)}) copy-start(f32[40,40,128]{2,1,0:T(8,128)} %param.19) | copy-start | bytes 2457604
  219.2 40.0 %copy-start.6 = (f32[40,128]{1,0:T(8,128)S(1)}, f32[40,128]{1,0:T(8,128)}, u32[]{:S(2)}) copy-start(f32[40,128]{1,0:T(8,128)} %param.18) | copy-start | bytes 61444
  228.9 213.8 %all-gather.7.cloned.1.call-start = ((), (), s32[]{:S(2)}) async-start(), calls=%async_computation.5 | async-start | bytes 2048000 | tf_op jit(solution)/shard_map/all_gather | solution.py:89
  253.8 5.4 %copy-start.2 = (bf16[40,40,128]{2,1,0:T(8,128)(2,1)}, bf16[40,40,128]{2,1,0:T(8,128)(2,1)S(1)}, u32[]{:S(2)}) copy-start(bf16[40,40,128]{2,1,0:T(8,128)(2,1)S(1)} %reduce_sum.56) | copy-start | bytes 1228804
  413.7 30.8 %copy-start.1 = (f32[40,40,128]{2,1,0:T(8,128)S(1)}, f32[40,40,128]{2,1,0:T(8,128)}, u32[]{:S(2)}) copy-start(f32[40,40,128]{2,1,0:T(8,128)} %param.19) | copy-start | bytes 2457604
  413.7 30.8 %copy-start.3 = (bf16[40,40,128]{2,1,0:T(8,128)(2,1)S(1)}, bf16[40,40,128]{2,1,0:T(8,128)(2,1)}, u32[]{:S(2)}) copy-start(bf16[40,40,128]{2,1,0:T(8,128)(2,1)} %copy-done.2) | copy-start | bytes 1228804
  413.7 30.8 %copy-start.4 = (bf16[40,40,128]{2,1,0:T(8,128)(2,1)S(1)}, bf16[40,40,128]{2,1,0:T(8,128)(2,1)}, u32[]{:S(2)}) copy-start(bf16[40,40,128]{2,1,0:T(8,128)(2,1)} %all-reduce.4.cloned.1.call-done) | copy-start | bytes 1228804
Sparse Core Ops, SparseCore 0:
  188.6 17.3 all-gather.4
  229.0 30.1 all-reduce.3
  425.3 17.2 all-gather.6
